TPU v7x, 32 devices: a whole 2x2x4 slice. The times are simulated.
32 devices in a mesh: aa: 8 (over y, x, core), ba: 4 (over z).
Axes of the slice: x: 2, y: 2, z: 4, core: 2. Of those that a mesh axis runs over, the one named last changes fastest.
Arguments:
- amplitudes: bfloat16 [1024, 2048], P('ba', 'aa'), may hold values from -6 to 6
- integrals: bfloat16 [512, 512, 2048], P('aa', 'ba'), may hold values from -0.125 to 0.125
- virt_energy: float32 [512], replicated, may hold values from 0.2 to 2
- pair_energy: float32 [1024], replicated, may hold values from 0.3 to 3
Outputs:
- update: float32 [512, 512, 1024], P('aa', 'ba')
All inputs are finite; a program needn't handle non-finite values.
Results may differ from a plain program's by a relative error of at most 0.0003.
Values may be sent and summed in bfloat16 or wider, within the bound.
A program may use at most 128 MiB of HBM per device.

v0:
```python
import jax
import jax.numpy as jnp
from jax import lax
from jax.sharding import PartitionSpec as P


def contract(left, right):
    return lax.dot_general(
        left, right, (((1,), (1,)), ((), ())), preferred_element_type=jnp.float32
    )


def on_device(amplitudes, integrals, virt_energy, pair_energy):
    first_count = integrals.shape[0]
    second_count = integrals.shape[1]
    cd_count = integrals.shape[2]
    flat_ints = integrals.reshape(first_count * second_count, cd_count)
    all_rows = lax.all_gather(amplitudes, "ba", axis=0, tiled=True)
    whole = lax.all_gather(all_rows, "aa", axis=1, tiled=True)
    ladder = contract(flat_ints, whole)
    pair_total = ladder.shape[1]
    ladder = ladder.reshape(first_count, second_count, pair_total)
    first_energy = lax.dynamic_slice_in_dim(
        virt_energy, lax.axis_index("aa") * first_count, first_count, 0
    )
    second_energy = lax.dynamic_slice_in_dim(
        virt_energy, lax.axis_index("ba") * second_count, second_count, 0
    )
    denom = first_energy[:, None, None] + second_energy[None, :, None] + pair_energy[None, None, :]
    return ladder / denom


def solution(mesh):
    placed = (P("ba", "aa"), P("aa", "ba", None), P(), P())
    return jax.shard_map(
        on_device, mesh=mesh, in_specs=placed, out_specs=P("aa", "ba", None), check_vma=False
    )
```

profile of v0, /device:TPU:0, one launch (start us, length us, event | category | flops | bytes accessed | tf_op | source)
XLA Modules:
  0.0 112.0 jit_solution(7729294179379284813)
XLA Ops:
  6.5 0.0 all-gather.2.cloned.1.call-start
  6.5 19.4 %all_gather.6 = bf16[1024,256]{1,0:T(8,128)(2,1)} all-gather(bf16[256,256]{1,0:T(8,128)(2,1)} %param.4), channel_id=1, replica_groups=mesh['aa'=8,'ba'=4] {'ba'}, dimensions={0}, use_global_device_ids=true | all-gather | bytes 655360 | tf_op jit(solution)/shard_map/all_gather | solution.py:18
  25.9 0.0 all-gather.2.cloned.1.call-update
  25.9 0.8 dynamic_slice.7
  26.7 0.8 dynamic_slice.6
  27.4 0.1 broadcast_add_fusion
  27.5 35.6 %all-gather.2.cloned.1.call-done = bf16[1024,2048]{1,0:T(8,128)(2,1)} async-done(((bf16[1024,256]{1,0:T(8,128)(2,1)}), bf16[1024,2048]{1,0:T(8,128)(2,1)}) %all-gather.2.cloned.1.call-update) | async-done | bytes 4194320 | tf_op jit(solution)/shard_map/all_gather | solution.py:19
  63.1 42.0 %add_divide_fusion = f32[64,128,1024]{2,1,0:T(8,128)} fusion(f32[1024]{0:T(1024)} %param.7, f32[64,128]{1,0:T(8,128)S(1)} %broadcast_add_fusion, bf16[64,128,2048]{2,1,0:T(8,128)(2,1)} %param.5, bf16[1024,2048]{1,0:T(8,128)(2,1)} %all-gather.2.cloned.1.call-done), kind=kOutput, calls=%fused_computation | convolution fusion | flops 34376515584 | bytes 71340032 | tf_op jit(solution)/shard_map/dot_general | solution.py:8
Async XLA Ops:
  6.5 56.6 %all-gather.2.cloned.1.call-start = ((), (), s32[]{:S(2)}) async-start(), calls=%async_computation | async-start | bytes 4718592 | tf_op jit(solution)/shard_map/all_gather | solution.py:19
Sparse Core Ops, SparseCore 0:
  26.0 37.0 all-gather.1
where the time goes:
time: 112 us
  matrix products  42 us (38%)
  waiting for transfers between devices  35.6 us (32%)
  blocking collectives  19.4 us (17%)
  between operations  13.4 us (12%)
  local copies, waits for them, and re-layouts  1.51 us (1%)
    dot_general x1, matrix products, contract(): lax.dot_general(left, right, (((1,), (1,)), ((), ())), preferred_element_...  42 us
    all_gather x1, waiting for transfers between devices, on_device(): whole = lax.all_gather(all_rows, 'aa', axis=1, tiled=True)  35.6 us
    all_gather x1, blocking collectives, on_device(): all_rows = lax.all_gather(amplitudes, 'ba', axis=0, tiled=True)  19.4 us
  transfers between devices with their start and end apart: 1, of which 1 were waited for; matrix products, arithmetic and copies ran while one was open for 1% of the time, Pallas kernels for 0%

commit v1 on v0

--- a/solution.py
+++ b/solution.py
@@ -16,7 +16,14 @@
     cd_count = integrals.shape[2]
     flat_ints = integrals.reshape(first_count * second_count, cd_count)
     all_rows = lax.all_gather(amplitudes, "ba", axis=0, tiled=True)
-    whole = lax.all_gather(all_rows, "aa", axis=1, tiled=True)
+    ways, here = (lax.axis_size("aa"), lax.axis_index("aa"))
+    whole, reach = (all_rows, 1)
+    while reach < ways:
+        theirs = lax.ppermute(whole, "aa", [(d, d ^ reach) for d in range(ways)])
+        mine_first = jnp.concatenate([whole, theirs], axis=1)
+        theirs_first = jnp.concatenate([theirs, whole], axis=1)
+        whole = jnp.where(here & reach == 0, mine_first, theirs_first)
+        reach = 2 * reach
     ladder = contract(flat_ints, whole)
     pair_total = ladder.shape[1]
     ladder = ladder.reshape(first_count, second_count, pair_total)

time: 112 us -> 195 us (1.74)
  waiting for transfers between devices: 35.6 us -> 70.9 us
  local copies, waits for them, and re-layouts: 1.51 us -> 33.6 us
  other arithmetic: 0.07 us -> 26.2 us
  between operations: 13.4 us -> 0.02 us
  starting transfers between devices: 0.01 us -> 3.14 us
    ppermute x0 -> x3, waiting for transfers between devices: none -> 70.9 us  [on_device(): theirs = lax.ppermute(whole, 'aa', [(d, d ^ reach) for d in range(ways)])]
    all_gather x1 -> x0, waiting for transfers between devices: 35.6 us -> none  [on_device(): whole = lax.all_gather(all_rows, 'aa', axis=1, tiled=True)]
    reshape x0 -> x1, local copies, waits for them, and re-layouts: none -> 33.5 us  [on_device(): ladder = ladder.reshape(first_count, second_count, pair_total)]
    div x0 -> x1, other arithmetic: none -> 23.6 us  [on_device(): return ladder / denom]
    ppermute x0 -> x3, starting transfers between devices: none -> 3.14 us  [on_device(): theirs = lax.ppermute(whole, 'aa', [(d, d ^ reach) for d in range(ways)])]
    select_n x0 -> x2, other arithmetic: none -> 2.53 us  [on_device(): whole = jnp.where(here & reach == 0, mine_first, theirs_first)]
  transfers between devices with their start and end apart: 1 -> 3, of which waited for: 1 -> 3; matrix products, arithmetic and copies ran while one was open for 1% -> 0% of each run, Pallas kernels for 0% -> 0%
where the time goes in v1:
time: 195 us; the launch traced here: 194 us
  waiting for transfers between devices  70.9 us (36%)
  matrix products  42.8 us (22%)
  local copies, waits for them, and re-layouts  33.6 us (17%)
  other arithmetic  26.2 us (13%)
  blocking collectives  17.7 us (9%)
  starting transfers between devices  3.14 us (2%)
    ppermute x3, waiting for transfers between devices, on_device(): theirs = lax.ppermute(whole, 'aa', [(d, d ^ reach) for d in range(ways)])  70.9 us
    dot_general x1, matrix products, contract(): lax.dot_general(left, right, (((1,), (1,)), ((), ())), preferred_element_...  42.8 us
    reshape x1, local copies, waits for them, and re-layouts, on_device(): ladder = ladder.reshape(first_count, second_count, pair_total)  33.5 us
    div x1, other arithmetic, on_device(): return ladder / denom  23.6 us
    all_gather x1, blocking collectives, on_device(): all_rows = lax.all_gather(amplitudes, 'ba', axis=0, tiled=True)  17.7 us
  transfers between devices with their start and end apart: 3, of which 3 were waited for; matrix products, arithmetic and copies ran while one was open for 0% of the time, Pallas kernels for 0%

profile of v1, /device:TPU:0, one launch (start us, length us, event | category | flops | bytes accessed | tf_op | source)
XLA Modules:
  0.0 194.4 jit_solution(3778121088974256673)
XLA Ops:
  0.0 0.0 copy-start.1
  0.0 17.7 %all_gather.3 = bf16[1024,256]{1,0:T(8,128)(2,1)S(1)} all-gather(bf16[256,256]{1,0:T(8,128)(2,1)} %param.4), channel_id=1, replica_groups=mesh['aa'=8,'ba'=4] {'ba'}, dimensions={0}, use_global_device_ids=true | all-gather | bytes 655360 | tf_op jit(solution)/shard_map/all_gather | solution.py:18
  17.7 0.0 collective-permute-start
  17.7 1.9 collective-permute-done
  19.6 0.2 maximum_select_fusion.3
  19.9 1.6 collective-permute-start.1
  21.4 23.8 %collective-permute-done.1 = bf16[1024,512]{1,0:T(8,128)(2,1)} collective-permute-done((bf16[1024,512]{1,0:T(8,128)(2,1)S(1)}, bf16[1024,512]{1,0:T(8,128)(2,1)}, u32[]{:S(2)}, u32[]{:S(2)}) %collective-permute-start.1) | collective-permute-done | bytes 1048608 | tf_op jit(solution)/shard_map/ppermute | solution.py:22
  45.2 2.3 %maximum_select_fusion.2 = bf16[1024,1024]{1,0:T(8,128)(2,1)S(1)} fusion(bf16[1024,512]{1,0:T(8,128)(2,1)} %collective-permute-done.1, bf16[1024,512]{1,0:T(8,128)(2,1)S(1)} %maximum_select_fusion.3, pred[]{:T(512)S(6)} %eq.10), kind=kLoop, calls=%fused_computation.9 | loop fusion | flops 9437184 | bytes 4194305 | tf_op jit(solution)/shard_map/jit(_where)/select_n | solution.py:25
  47.5 1.6 collective-permute-start.2
  49.1 0.0 copy-done.1
  49.1 0.1 dynamic_slice.7
  49.2 0.1 dynamic_slice.6
  49.3 0.1 broadcast_add_fusion
  49.3 45.2 %collective-permute-done.2 = bf16[1024,1024]{1,0:T(8,128)(2,1)} collective-permute-done((bf16[1024,1024]{1,0:T(8,128)(2,1)S(1)}, bf16[1024,1024]{1,0:T(8,128)(2,1)}, u32[]{:S(2)}, u32[]{:S(2)}) %collective-permute-start.2) | collective-permute-done | bytes 2097184 | tf_op jit(solution)/shard_map/ppermute | solution.py:22
  94.5 42.8 %convolution_bitcast_fusion = f32[8192,1024]{0,1:T(8,128)} fusion(bf16[8192,2048]{1,0:T(8,128)(2,1)} %bitcast.6, bf16[1024,1024]{1,0:T(8,128)(2,1)} %collective-permute-done.2, bf16[1024,1024]{1,0:T(8,128)(2,1)S(1)} %maximum_select_fusion.2, pred[]{:T(512)S(6)} %eq.9), kind=kOutput, calls=%fused_computation.1 | convolution fusion | flops 34378612736 | bytes 71303168 | tf_op jit(solution)/shard_map/dot_general | solution.py:8
  137.3 0.0 copy-start
  137.3 33.5 %copy.6 = f32[8192,1024]{1,0:T(8,128)} copy(f32[8192,1024]{0,1:T(8,128)} %convolution_bitcast_fusion) | data formatting | bytes 67108864 | tf_op jit(solution)/shard_map/reshape | solution.py:29
  170.8 0.0 copy-done
  170.8 23.6 %add_divide_fusion = f32[64,128,1024]{2,1,0:T(8,128)} fusion(f32[64,128,1024]{2,1,0:T(8,128)} %bitcast.5, f32[1024]{0:T(1024)S(1)} %copy-done, f32[64,128]{1,0:T(8,128)S(1)} %broadcast_add_fusion), kind=kLoop, calls=%fused_computation | loop fusion | flops 16777216 | bytes 67145728 | tf_op jit(solution)/shard_map/div | solution.py:37
Async XLA Ops:
  0.0 49.1 %copy-start.1 = (f32[512]{0:T(512)S(1)}, f32[512]{0:T(512)}, u32[]{:S(2)}) copy-start(f32[512]{0:T(512)} %param.6) | copy-start | bytes 6148
  17.7 1.9 collective-permute-start
  19.9 25.4 %collective-permute-start.1 = (bf16[1024,512]{1,0:T(8,128)(2,1)S(1)}, bf16[1024,512]{1,0:T(8,128)(2,1)}, u32[]{:S(2)}, u32[]{:S(2)}) collective-permute-start(bf16[1024,512]{1,0:T(8,128)(2,1)S(1)} %maximum_select_fusion.3), channel_id=1, source_target_pairs={{0,8},{4,12},{8,0},{12,4},{16,24},{20,28},{24,16},{28,20},{1,9},{5... | collective-permute-start | bytes 3145736 | tf_op jit(solution)/shard_map/ppermute | solution.py:22
  47.5 47.0 %collective-permute-start.2 = (bf16[1024,1024]{1,0:T(8,128)(2,1)S(1)}, bf16[1024,1024]{1,0:T(8,128)(2,1)}, u32[]{:S(2)}, u32[]{:S(2)}) collective-permute-start(bf16[1024,1024]{1,0:T(8,128)(2,1)S(1)} %maximum_select_fusion.2), channel_id=1, source_target_pairs={{0,16},{4,20},{8,24},{12,28},{16,0},{20,4},{24,8},{28,12},{1,17},{... | collective-permute-start | bytes 6291464 | tf_op jit(solution)/shard_map/ppermute | solution.py:22
  137.3 33.5 %copy-start = (f32[1024]{0:T(1024)S(1)}, f32[1024]{0:T(1024)}, u32[]{:S(2)}) copy-start(f32[1024]{0:T(1024)} %param.7) | copy-start | bytes 12292
